TPU v7x, 512 devices: a whole 4x4x16 slice. The times are simulated.
512 devices in a mesh: rows: 64 (over x_lo, z, core), blk: 8 (over x_hi, y).
Axes of the slice: x: 4 (x_hi: 2, x_lo: 2; x = x_hi * 2 + x_lo), y: 4, z: 16, core: 2. Of those that a mesh axis runs over, the one named last changes fastest.
Arguments:
- cov_blocks: bfloat16 [1024, 40, 128, 128], P(('rows', 'blk')), may hold values from -24 to 24
- col_index: int32 [1024, 40], P(('rows', 'blk')), may hold values from 0 to 1023, as said below
- block_count: int32 [1024], P(('rows', 'blk')), may hold values from 2 to 40, as said below
- probes: bfloat16 [131072, 512], P(('rows', 'blk')), may hold values from -60 to 60
Outputs:
- basis: float32 [131072, 512], P(('rows', 'blk'))
Inputs may be any that keep to these rules, and one draw needn't show every extreme that they name: `col_index`: the live slots of block row i name distinct column blocks of zone i // 16 or of an adjacent zone; rows of the first and last zone have at most 32 live slots; every entry of a row is distinct. `block_count`: some block row uses all 40 slots in every draw.
All inputs are finite; a program needn't handle non-finite values.
Results may differ from a plain program's by a relative error of at most 0.0003.
Values may be sent and summed in bfloat16 or wider, within the bound.
A program may use at most 64 MiB of HBM per device.

v0:
```python
import jax
import jax.numpy as jnp
from jax import lax
from jax.sharding import PartitionSpec as P


def extended(x, sides, width):
    for axis, dim in sides:
        devices, length = (lax.axis_size(axis), x.shape[dim])
        up = [(i, (i + 1) % devices) for i in range(devices - 1)]
        down = [(j, i) for i, j in up]
        last = lax.slice_in_dim(x, length - width, length, axis=dim)
        first = lax.slice_in_dim(x, 0, width, axis=dim)
        before = lax.ppermute(last, axis, up)
        after = lax.ppermute(first, axis, down)
        x = jnp.concatenate([before, x, after], axis=dim)
    return x


def local(cov_blocks, col_index, block_count, probes):
    rows_here, slots, block, _ = cov_blocks.shape
    tile_rows = probes.shape[0]
    probe_cols = probes.shape[1]
    zone_blocks = rows_here * lax.axis_size("blk")
    zone_number = lax.axis_index("rows")
    relative = col_index - (zone_number - 1) * zone_blocks
    window_blocks = 3 * zone_blocks
    inside = (relative >= 0) & (relative < window_blocks)
    slot_ids = lax.broadcasted_iota(jnp.int32, (rows_here, slots), 1)
    live_mask = inside & (slot_ids < block_count[:, None])
    column_ids = jnp.arange(window_blocks, dtype=jnp.int32)
    hits = (relative[:, :, None] == column_ids[None, None, :]) & live_mask[:, :, None]
    selector = hits.astype(jnp.bfloat16)
    window_matrix = jnp.einsum(
        "lsp,lsac->lapc", selector, cov_blocks, preferred_element_type=jnp.float32
    )
    window_matrix = window_matrix.astype(jnp.bfloat16).reshape(
        rows_here * block, window_blocks * block
    )

    def add_columns(running, shard_rows, first_row):
        length = shard_rows.shape[0]
        columns = lax.dynamic_slice_in_dim(window_matrix, first_row, length, 1)
        return running + jnp.dot(columns, shard_rows, preferred_element_type=jnp.float32)

    zeros_out = jnp.zeros((tile_rows, probe_cols), jnp.float32)
    own_zone = lax.all_gather(probes, "blk", axis=0, tiled=True)
    zone_length = own_zone.shape[0]
    images = add_columns(zeros_out, own_zone, zone_length)
    near_zones = extended(own_zone, (("rows", 0),), zone_length)
    images = add_columns(images, lax.slice_in_dim(near_zones, 0, zone_length, axis=0), 0)
    images = add_columns(
        images,
        lax.slice_in_dim(near_zones, 2 * zone_length, 3 * zone_length, axis=0),
        2 * zone_length,
    )
    gram_local = lax.dot_general(
        images,
        images,
        (((0,), (0,)), ((), ())),
        precision=lax.Precision.HIGHEST,
        preferred_element_type=jnp.float32,
    )
    gram_total = lax.psum(gram_local, ("rows", "blk"))
    point_count = tile_rows * lax.axis_size("rows") * lax.axis_size("blk")
    gram_matrix = gram_total / point_count
    factor = jnp.linalg.cholesky(gram_matrix)
    return lax.linalg.triangular_solve(
        factor, images, left_side=False, lower=True, transpose_a=True
    )


def solution(mesh):
    return jax.shard_map(
        local,
        mesh=mesh,
        in_specs=(
            P(("rows", "blk"), None, None, None),
            P(("rows", "blk"), None),
            P(("rows", "blk")),
            P(("rows", "blk"), None),
        ),
        out_specs=P(("rows", "blk"), None),
        check_vma=False,
    )
```

profile of v0, /device:TPU:1, one launch (start us, length us, event | category | flops | bytes accessed | tf_op | source)
XLA Modules:
  0.0 755.8 jit_solution(5842420707224924274)
XLA Ops:
  6.5 0.7 all-gather.2.cloned.1.call-update
  7.3 77.5 %all-gather.2.cloned.1.call-done = bf16[2048,512]{1,0:T(8,128)(2,1)} async-done(((bf16[256,512]{1,0:T(8,128)(2,1)}), bf16[2048,512]{1,0:T(8,128)(2,1)}) %all-gather.2.cloned.1.call-update) | async-done | bytes 2097168 | tf_op jit(solution)/shard_map/all_gather | solution.py:47
  84.8 4.1 collective-permute-start
  89.0 1.9 collective-permute-start.1
  90.9 0.8 compare_and_fusion
  91.7 2.7 fusion.2
  94.4 0.8 copy.17
  95.2 0.8 copy-done.2
  96.0 0.7 fusion.7
  96.7 15.6 %collective-permute-done = bf16[2048,512]{1,0:T(8,128)(2,1)} collective-permute-done((bf16[2048,512]{1,0:T(8,128)(2,1)}, bf16[2048,512]{1,0:T(8,128)(2,1)}, u32[]{:S(2)}, u32[]{:S(2)}) %collective-permute-start) | collective-permute-done | bytes 2097184 | tf_op jit(solution)/shard_map/ppermute | solution.py:14
  112.3 2.3 convolution_add_fusion.1
  114.6 2.1 collective-permute-done.1
  116.7 2.3 convolution_add_fusion
  119.0 2.1 fusion.48
  121.1 464.7 %all-reduce.3.cloned.1.call-done = f32[512,512]{0,1:T(8,128)} async-done(((f32[512,512]{0,1:T(8,128)}), f32[512,512]{0,1:T(8,128)}) %all-reduce.3.cloned.1.call-update) | async-done | bytes 1048592 | tf_op jit(solution)/shard_map/psum | solution.py:64
  585.8 2.3 broadcast_multiply_fusion
  588.1 2.6 copy.7
  590.7 1.8 fusion.9
  592.5 1.0 copy-done.1
  593.5 11.7 %cholesky.104 = f32[128,128]{1,0:T(8,128)S(1)} custom-call(f32[128,128]{1,0:T(8,128)S(1)} %cholesky.266), custom_call_target="Cholesky" | custom-call | tf_op jit(solution)/shard_map/jit(cholesky)/cholesky | solution.py:67
  605.2 9.8 %custom-call.30 = f32[1,128,128]{1,2,0:T(8,128)S(1)} custom-call(f32[1,128,128]{2,1,0:T(8,128)S(1)} %get-tuple-element.34), custom_call_target="InvertDiagBlocksLowerTriangular" | custom-call | tf_op jit(solution)/shard_map/jit(cholesky)/cholesky | solution.py:67
  615.1 1.2 cholesky.224
  616.2 2.1 constant_dynamic-update-slice_fusion.3
  618.4 1.3 convolution_subtract_fusion
  619.6 11.7 %cholesky.217 = f32[128,128]{1,0:T(8,128)S(1)} custom-call(f32[128,128]{1,0:T(8,128)S(1)} %cholesky.270), custom_call_target="Cholesky" | custom-call | tf_op jit(solution)/shard_map/jit(cholesky)/cholesky | solution.py:67
  631.4 0.6 select_reduce_fusion.2
  632.0 9.8 %custom-call.31 = f32[1,128,128]{1,2,0:T(8,128)S(1)} custom-call(f32[1,128,128]{2,1,0:T(8,128)S(1)} %get-tuple-element.31), custom_call_target="InvertDiagBlocksLowerTriangular" | custom-call | tf_op jit(solution)/shard_map/jit(cholesky)/cholesky | solution.py:67
  641.8 0.9 convolution_dynamic-update-slice_fusion
  642.8 1.4 convolution_subtract_fusion.1
  644.2 11.7 %cholesky.238 = f32[128,128]{1,0:T(8,128)S(1)} custom-call(f32[128,128]{1,0:T(8,128)S(1)} %cholesky.275), custom_call_target="Cholesky" | custom-call | tf_op jit(solution)/shard_map/jit(cholesky)/cholesky | solution.py:67
  656.6 0.6 compare_reduce_fusion.1
  657.2 10.0 %custom-call.32 = f32[1,128,128]{1,2,0:T(8,128)S(1)} custom-call(f32[1,128,128]{2,1,0:T(8,128)S(1)} %get-tuple-element.28), custom_call_target="InvertDiagBlocksLowerTriangular" | custom-call | tf_op jit(solution)/shard_map/jit(cholesky)/cholesky | solution.py:67
  667.2 0.8 convolution_dynamic-update-slice_fusion.1
  668.0 1.4 convolution_subtract_fusion.2
  669.5 11.7 %cholesky.255 = f32[128,128]{1,0:T(8,128)S(1)} custom-call(f32[128,128]{1,0:T(8,128)S(1)} %convolution_subtract_fusion.2), custom_call_target="Cholesky" | custom-call | tf_op jit(solution)/shard_map/jit(cholesky)/cholesky | solution.py:67
  681.2 0.7 select_reduce_fusion
  681.8 0.7 compare_reduce_fusion
  685.5 2.4 select_select_fusion
  687.9 14.1 %while.1 = (s32[]{:T(128)}, f32[512,512]{1,0:T(8,128)}, s32[4,2]{0,1:T(2,128)S(1)}, f32[4,128,128]{2,1,0:T(8,128)}, s32[]{:T(128)}) while((s32[]{:T(128)}, f32[512,512]{1,0:T(8,128)}, s32[4,2]{0,1:T(2,128)S(1)}, f32[4,128,128]{2,1,0:T(8,128)}, s32[]{:T(128)}) %tuple.28), condition=%wide.while_cond, body=%wide.while_body.sunk | while | flops 2 | bytes 132705 | solution.py:68
  688.6 2.9 bitcast_dynamic-update-slice_fusion.2
  692.1 2.9 bitcast_dynamic-update-slice_fusion.2
  695.7 2.9 bitcast_dynamic-update-slice_fusion.2
  699.2 2.8 bitcast_dynamic-update-slice_fusion.2
  702.0 40.1 %custom-call.33 = f32[4,128,128]{1,2,0:T(8,128)S(1)} custom-call(f32[4,128,128]{2,1,0:T(8,128)} %get-tuple-element.12), custom_call_target="InvertDiagBlocksLowerTriangular" | custom-call | tf_op jit(solution)/shard_map/triangular_solve | solution.py:68
  742.5 1.2 fusion.33
  744.0 1.5 fusion.17
  745.9 1.7 fusion.10
  748.0 1.0 copy.8
  (29 shorter events, 5.4 us)
Async XLA Ops:
  6.5 85.2 %copy-start = (bf16[2,40,128,128]{3,2,1,0:T(8,128)(2,1)S(1)}, bf16[2,40,128,128]{3,2,1,0:T(8,128)(2,1)}, u32[]{:S(2)}) copy-start(bf16[2,40,128,128]{3,2,1,0:T(8,128)(2,1)} %param.4) | copy-start | bytes 7864324
  6.5 78.3 %all-gather.2.cloned.1.call-start = ((), (), s32[]{:S(2)}) async-start(), calls=%async_computation | async-start | bytes 2359296 | tf_op jit(solution)/shard_map/all_gather | solution.py:47
  7.3 578.6 %all-reduce.3.cloned.1.call-start = ((), (), s32[]{:S(2)}) async-start(), calls=%async_computation.1 | async-start | bytes 2097152 | tf_op jit(solution)/shard_map/psum | solution.py:64
  84.8 27.4 %collective-permute-start = (bf16[2048,512]{1,0:T(8,128)(2,1)}, bf16[2048,512]{1,0:T(8,128)(2,1)}, u32[]{:S(2)}, u32[]{:S(2)}) collective-permute-start(bf16[2048,512]{1,0:T(8,128)(2,1)} %all-gather.2.cloned.1.call-done), channel_id=1, source_target_pairs={{0,8},{8,16},{16,24},{24,32},{32,40},{40,48},{48,56},{56,64},{64,7... | collective-permute-start | bytes 6291464 | tf_op jit(solution)/shard_map/ppermute | solution.py:14
  89.0 27.7 %collective-permute-start.1 = (bf16[2048,512]{1,0:T(8,128)(2,1)}, bf16[2048,512]{1,0:T(8,128)(2,1)}, u32[]{:S(2)}, u32[]{:S(2)}) collective-permute-start(bf16[2048,512]{1,0:T(8,128)(2,1)} %all-gather.2.cloned.1.call-done), channel_id=1, source_target_pairs={{8,0},{16,8},{24,16},{32,24},{40,32},{48,40},{56,48},{64,56},{72,6... | collective-permute-start | bytes 6291464 | tf_op jit(solution)/shard_map/ppermute | solution.py:15
  94.4 1.6 copy-start.2
  592.5 1.0 copy-start.1
Sparse Core Ops, SparseCore 0:
  10.6 74.2 all-gather.1
  121.2 464.5 all-reduce.2
where the time goes:
time: 757 us; the launch traced here: 756 us
  waiting for transfers between devices  561 us (74%)
  other arithmetic  128 us (17%)
  matrix products  23.8 us (3%)
  local copies, waits for them, and re-layouts  21.5 us (3%)
  between operations  16 us (2%)
    psum x1, waiting for transfers between devices, local(): gram_total = lax.psum(gram_local, ('rows', 'blk'))  465 us
    another operation x14, other arithmetic, local(): factor = jnp.linalg.cholesky(gram_matrix)  80.4 us
    all_gather x1, waiting for transfers between devices, local(): own_zone = lax.all_gather(probes, 'blk', axis=0, tiled=True)  77.5 us
    another operation x4, other arithmetic, local(): lax.linalg.triangular_solve(factor, images, left_side=False, lower=True,...  42.5 us
    ppermute x1, waiting for transfers between devices, extended(): before = lax.ppermute(last, axis, up)  15.6 us
  transfers between devices with their start and end apart: 4, of which 4 were waited for; matrix products, arithmetic and copies ran while one was open for 1% of the time, Pallas kernels for 0%

commit v1 on v0

--- a/solution.py
+++ b/solution.py
@@ -1,7 +1,17 @@
+import functools
 import jax
 import jax.numpy as jnp
 from jax import lax
 from jax.sharding import PartitionSpec as P
+
+
+def stages_all_work(content, along_axis, device_axis):
+    for j0 in (along_axis, device_axis):
+        content = lax.psum(content, axis_name=j0)
+    return content
+
+
+arrange_spans_on_mesh = functools.partial(stages_all_work, along_axis="blk", device_axis="rows")
 
 
 def extended(x, sides, width):
@@ -61,7 +71,7 @@
         precision=lax.Precision.HIGHEST,
         preferred_element_type=jnp.float32,
     )
-    gram_total = lax.psum(gram_local, ("rows", "blk"))
+    gram_total = arrange_spans_on_mesh(gram_local)
     point_count = tile_rows * lax.axis_size("rows") * lax.axis_size("blk")
     gram_matrix = gram_total / point_count
     factor = jnp.linalg.cholesky(gram_matrix)

time: 757 us -> 826 us (1.091)
  waiting for transfers between devices: 561 us -> 630 us
    psum x1 -> x2, waiting for transfers between devices: 465 us -> 534 us  [stages_all_work(): content = lax.psum(content, axis_name=j0)]
  transfers between devices with their start and end apart: 4 -> 5, of which waited for: 4 -> 5; matrix products, arithmetic and copies ran while one was open for 1% -> 1% of each run, Pallas kernels for 0% -> 0%
where the time goes in v1:
time: 826 us
  waiting for transfers between devices  630 us (76%)
  other arithmetic  128 us (15%)
  matrix products  23.6 us (3%)
  local copies, waits for them, and re-layouts  21.5 us (3%)
  between operations  15.7 us (2%)
    psum x2, waiting for transfers between devices, stages_all_work(): content = lax.psum(content, axis_name=j0)  534 us
    another operation x14, other arithmetic, local(): factor = jnp.linalg.cholesky(gram_matrix)  80.6 us
    all_gather x1, waiting for transfers between devices, local(): own_zone = lax.all_gather(probes, 'blk', axis=0, tiled=True)  77.5 us
    another operation x4, other arithmetic, local(): lax.linalg.triangular_solve(factor, images, left_side=False, lower=True,...  42.5 us
  transfers between devices with their start and end apart: 5, of which 5 were waited for; matrix products, arithmetic and copies ran while one was open for 1% of the time, Pallas kernels for 0%

profile of v1, /device:TPU:1, one launch (start us, length us, event | category | flops | bytes accessed | tf_op | source)
XLA Modules:
  0.0 825.5 jit_solution(3335916607384475046)
XLA Ops:
  6.5 0.7 all-gather.2.cloned.1.call-update
  7.3 77.5 %all-gather.2.cloned.1.call-done = bf16[2048,512]{1,0:T(8,128)(2,1)} async-done(((bf16[256,512]{1,0:T(8,128)(2,1)}), bf16[2048,512]{1,0:T(8,128)(2,1)}) %all-gather.2.cloned.1.call-update) | async-done | bytes 2097168 | tf_op jit(solution)/shard_map/all_gather | solution.py:57
  84.8 4.1 collective-permute-start
  89.0 1.9 collective-permute-start.1
  90.9 0.8 compare_and_fusion
  91.7 2.7 fusion.2
  94.4 0.8 copy.17
  95.2 0.8 copy-done.2
  96.0 0.7 fusion.7
  96.7 15.6 %collective-permute-done = bf16[2048,512]{1,0:T(8,128)(2,1)} collective-permute-done((bf16[2048,512]{1,0:T(8,128)(2,1)}, bf16[2048,512]{1,0:T(8,128)(2,1)}, u32[]{:S(2)}, u32[]{:S(2)}) %collective-permute-start) | collective-permute-done | bytes 2097184 | tf_op jit(solution)/shard_map/ppermute | solution.py:24
  112.3 2.3 convolution_add_fusion.1
  114.6 2.1 collective-permute-done.1
  116.7 2.3 convolution_add_fusion
  119.0 2.0 fusion.48
  121.3 96.0 %all-reduce.4.cloned.1.call-done = f32[512,512]{0,1:T(8,128)} async-done(((f32[512,512]{0,1:T(8,128)}), f32[512,512]{0,1:T(8,128)}) %all-reduce.4.cloned.1.call-update) | async-done | bytes 1048592 | tf_op jit(solution)/shard_map/psum | solution.py:10
  217.3 438.4 %all-reduce.6.cloned.1.call-done = f32[512,512]{0,1:T(8,128)} async-done(((f32[512,512]{0,1:T(8,128)}), f32[512,512]{0,1:T(8,128)}) %all-reduce.6.cloned.1.call-update) | async-done | bytes 1048592 | tf_op jit(solution)/shard_map/psum | solution.py:10
  655.8 2.3 broadcast_multiply_fusion
  658.1 2.6 copy.7
  660.7 1.8 fusion.9
  662.5 1.0 copy-done.1
  663.5 11.7 %cholesky.104 = f32[128,128]{1,0:T(8,128)S(1)} custom-call(f32[128,128]{1,0:T(8,128)S(1)} %cholesky.266), custom_call_target="Cholesky" | custom-call | tf_op jit(solution)/shard_map/jit(cholesky)/cholesky | solution.py:77
  675.2 9.8 %custom-call.30 = f32[1,128,128]{1,2,0:T(8,128)S(1)} custom-call(f32[1,128,128]{2,1,0:T(8,128)S(1)} %get-tuple-element.34), custom_call_target="InvertDiagBlocksLowerTriangular" | custom-call | tf_op jit(solution)/shard_map/jit(cholesky)/cholesky | solution.py:77
  685.0 1.2 cholesky.224
  686.2 2.0 constant_dynamic-update-slice_fusion.3
  688.2 1.2 convolution_subtract_fusion
  689.4 11.7 %cholesky.217 = f32[128,128]{1,0:T(8,128)S(1)} custom-call(f32[128,128]{1,0:T(8,128)S(1)} %cholesky.270), custom_call_target="Cholesky" | custom-call | tf_op jit(solution)/shard_map/jit(cholesky)/cholesky | solution.py:77
  701.1 0.6 select_reduce_fusion.2
  701.8 10.0 %custom-call.31 = f32[1,128,128]{1,2,0:T(8,128)S(1)} custom-call(f32[1,128,128]{2,1,0:T(8,128)S(1)} %get-tuple-element.31), custom_call_target="InvertDiagBlocksLowerTriangular" | custom-call | tf_op jit(solution)/shard_map/jit(cholesky)/cholesky | solution.py:77
  711.8 0.9 convolution_dynamic-update-slice_fusion
  712.7 1.4 convolution_subtract_fusion.1
  714.2 11.7 %cholesky.238 = f32[128,128]{1,0:T(8,128)S(1)} custom-call(f32[128,128]{1,0:T(8,128)S(1)} %cholesky.275), custom_call_target="Cholesky" | custom-call | tf_op jit(solution)/shard_map/jit(cholesky)/cholesky | solution.py:77
  727.2 9.8 %custom-call.32 = f32[1,128,128]{1,2,0:T(8,128)S(1)} custom-call(f32[1,128,128]{2,1,0:T(8,128)S(1)} %get-tuple-element.28), custom_call_target="InvertDiagBlocksLowerTriangular" | custom-call | tf_op jit(solution)/shard_map/jit(cholesky)/cholesky | solution.py:77
  737.0 0.8 convolution_dynamic-update-slice_fusion.1
  737.8 1.4 convolution_subtract_fusion.2
  739.2 11.7 %cholesky.255 = f32[128,128]{1,0:T(8,128)S(1)} custom-call(f32[128,128]{1,0:T(8,128)S(1)} %convolution_subtract_fusion.2), custom_call_target="Cholesky" | custom-call | tf_op jit(solution)/shard_map/jit(cholesky)/cholesky | solution.py:77
  750.9 0.7 select_reduce_fusion
  751.6 0.9 compare_reduce_fusion
  755.6 2.4 select_select_fusion
  757.9 14.1 %while.1 = (s32[]{:T(128)}, f32[512,512]{1,0:T(8,128)}, s32[4,2]{0,1:T(2,128)S(1)}, f32[4,128,128]{2,1,0:T(8,128)}, s32[]{:T(128)}) while((s32[]{:T(128)}, f32[512,512]{1,0:T(8,128)}, s32[4,2]{0,1:T(2,128)S(1)}, f32[4,128,128]{2,1,0:T(8,128)}, s32[]{:T(128)}) %tuple.28), condition=%wide.while_cond, body=%wide.while_body.sunk | while | flops 2 | bytes 132705 | solution.py:78
  758.6 2.9 bitcast_dynamic-update-slice_fusion.2
  762.1 2.9 bitcast_dynamic-update-slice_fusion.2
  765.7 2.9 bitcast_dynamic-update-slice_fusion.2
  769.2 2.8 bitcast_dynamic-update-slice_fusion.2
  772.1 40.1 %custom-call.33 = f32[4,128,128]{1,2,0:T(8,128)S(1)} custom-call(f32[4,128,128]{2,1,0:T(8,128)} %get-tuple-element.12), custom_call_target="InvertDiagBlocksLowerTriangular" | custom-call | tf_op jit(solution)/shard_map/triangular_solve | solution.py:78
  812.5 1.2 fusion.33
  814.1 1.5 fusion.17
  815.9 1.7 fusion.10
  818.0 1.0 copy.8
  (32 shorter events, 6.3 us)
Async XLA Ops:
  6.5 85.2 %copy-start = (bf16[2,40,128,128]{3,2,1,0:T(8,128)(2,1)S(1)}, bf16[2,40,128,128]{3,2,1,0:T(8,128)(2,1)}, u32[]{:S(2)}) copy-start(bf16[2,40,128,128]{3,2,1,0:T(8,128)(2,1)} %param.4) | copy-start | bytes 7864324
  6.5 78.3 %all-gather.2.cloned.1.call-start = ((), (), s32[]{:S(2)}) async-start(), calls=%async_computation | async-start | bytes 2359296 | tf_op jit(solution)/shard_map/all_gather | solution.py:57
  7.3 210.0 %all-reduce.4.cloned.1.call-start = ((), (), s32[]{:S(2)}) async-start(), calls=%async_computation.1 | async-start | bytes 2097152 | tf_op jit(solution)/shard_map/psum | solution.py:10
  84.8 27.4 %collective-permute-start = (bf16[2048,512]{1,0:T(8,128)(2,1)}, bf16[2048,512]{1,0:T(8,128)(2,1)}, u32[]{:S(2)}, u32[]{:S(2)}) collective-permute-start(bf16[2048,512]{1,0:T(8,128)(2,1)} %all-gather.2.cloned.1.call-done), channel_id=1, source_target_pairs={{0,8},{8,16},{16,24},{24,32},{32,40},{40,48},{48,56},{56,64},{64,7... | collective-permute-start | bytes 6291464 | tf_op jit(solution)/shard_map/ppermute | solution.py:24
  89.0 27.7 %collective-permute-start.1 = (bf16[2048,512]{1,0:T(8,128)(2,1)}, bf16[2048,512]{1,0:T(8,128)(2,1)}, u32[]{:S(2)}, u32[]{:S(2)}) collective-permute-start(bf16[2048,512]{1,0:T(8,128)(2,1)} %all-gather.2.cloned.1.call-done), channel_id=1, source_target_pairs={{8,0},{16,8},{24,16},{32,24},{40,32},{48,40},{56,48},{64,56},{72,6... | collective-permute-start | bytes 6291464 | tf_op jit(solution)/shard_map/ppermute | solution.py:25
  94.4 1.6 copy-start.2
  121.0 534.8 %all-reduce.6.cloned.1.call-start = ((), (), s32[]{:S(2)}) async-start(), calls=%async_computation.2 | async-start | bytes 2097152 | tf_op jit(solution)/shard_map/psum | solution.py:10
  662.5 1.0 copy-start.1
Sparse Core Ops, SparseCore 0:
  10.6 74.2 all-gather.1
  121.1 96.1 all-reduce.3
  220.2 435.5 all-reduce.5
